TPU v7x, 256 devices: a whole 4x4x8 slice. The times are simulated.
256 devices in a mesh: tok: 8 (over z), out: 16 (over y_lo, x, core), grp: 2 (over y_hi).
Axes of the slice: x: 4, y: 4 (y_hi: 2, y_lo: 2; y = y_hi * 2 + y_lo), z: 8, core: 2. Of those that a mesh axis runs over, the one named last changes fastest.
Arguments:
- activations: bfloat16 [2048, 2, 2048], P(('tok', 'grp'), None, 'out'), may hold values from -16 to 16
- out_grads: bfloat16 [2048, 2, 2048], P(('tok', 'grp'), None, 'out'), may hold values from -16 to 16
- weight: bfloat16 [2, 2048, 4096], P(None, 'out'), may hold values from -0.09375 to 0.09375
Outputs:
- update: bfloat16 [4096, 2, 2048], P(('tok', 'grp'), None, 'out')
- input_grad: bfloat16 [2048, 2, 2048], P(('tok', 'grp'), None, 'out')
All inputs are finite; a program needn't handle non-finite values.
Results may differ from a plain program's by a relative error of at most 0.0092.
Values may be sent and summed in bfloat16 or wider, within the bound.
No kernel may reach another device: no remote copies, remote signals or barrier semaphores. Data moves between devices by JAX's collectives and lax.ppermute only.
A program may use at most 64 MiB of HBM per device.

v0:
```python
import math
import jax
import jax.numpy as jnp
from jax import lax
from jax.sharding import Mesh
from jax.sharding import PartitionSpec as P

POWER = 3
OUT = ("out_0", "out_1", "out_2")
TOK_OUT = ("tok", "out_0", "out_1", "out_2")
DAMPING = 0.1
HIGH = lax.Precision.HIGHEST


def own_rows(so_far, axes):
    for axis in axes:
        so_far = lax.psum_scatter(so_far, axis, scatter_dimension=0, tiled=True)
    return so_far


def in_order(pieces, dim):
    lengths = list(pieces.shape[1:])
    lengths[dim] *= pieces.shape[0]
    return jnp.moveaxis(pieces, 0, dim).reshape(lengths)


def copy_for_each(array, axis):
    peers = lax.axis_size(axis)
    return lax.all_to_all(
        jnp.broadcast_to(array[None], (peers, *array.shape)), axis, 0, 0, tiled=True
    )


def gather_directly(array, axis, dim):
    return in_order(copy_for_each(array, axis), dim)


def one_axis_at_a_time(array, axes):
    for axis in axes:
        array = lax.psum(array, axis)
    return array


def swapped(array, axis, stride):
    return lax.ppermute(array, axis, [(i, i ^ 1 << stride) for i in range(lax.axis_size(axis))])


def spread(piece):
    return lax.all_gather(piece, OUT, axis=2, tiled=True)


def token_sums(maker, rows):
    return own_rows(maker(jnp.int32(0), rows * lax.axis_size(("tok", "grp"))), ("tok", "grp"))


def owner_rows(piece):
    return gather_directly(piece, "tok", 0)


def owner_total(vector):
    return one_axis_at_a_time(vector, TOK_OUT)


def diagonal_mask(rows, width, row_start, col_start):
    row_ids = row_start + lax.broadcasted_iota(jnp.int32, (rows, 1, width), 0)
    col_ids = col_start + lax.broadcasted_iota(jnp.int32, (rows, 1, width), 2)
    return jnp.where(row_ids == col_ids, 1.0, 0.0).astype(jnp.float32)


def multiply(left, right, gather_columns):
    row_band = spread(left)
    column_band = gather_columns(right)
    return jnp.einsum("rkj,jkc->rkc", row_band, column_band, preferred_element_type=jnp.float32)


def inverse_roots(tile, row_start, col_start, gather_columns, total):
    rows, count, width = tile.shape
    block = width * lax.axis_size(OUT)
    mask = diagonal_mask(rows, width, row_start, col_start)
    vector = jnp.ones((count, block), jnp.float32)
    image = vector
    for step in range(POWER):
        columns = lax.dynamic_slice_in_dim(vector, col_start, width, 1)
        part = jnp.einsum("rkc,kc->kr", tile, columns, precision=HIGH)
        placed = lax.dynamic_update_slice_in_dim(
            jnp.zeros((count, block), jnp.float32), part, row_start, 1
        )
        image = total(placed)
        if step + 1 < POWER:
            vector = image / jnp.sqrt(jnp.sum(image * image, axis=1, keepdims=True))
    scale = jnp.sum(vector * image, axis=1) / jnp.sum(vector * vector, axis=1)
    start = tile / scale[None, :, None]
    start_low = start.astype(jnp.bfloat16)
    first_low = ((3.0 * mask - start) / 2.0).astype(jnp.bfloat16)
    square_low = multiply(first_low, first_low, gather_columns).astype(jnp.bfloat16)
    moved = multiply(square_low, start_low, gather_columns)
    second_low = ((3.0 * mask - moved) / 2.0).astype(jnp.bfloat16)
    roots = multiply(first_low, second_low, gather_columns) / jnp.sqrt(scale)[None, :, None]
    return roots.astype(jnp.bfloat16)


def local(activations, out_grads, weight):
    tok_dev, blocks, width = activations.shape
    block = width * lax.axis_size(OUT)
    token_count = tok_dev * lax.axis_size("tok") * lax.axis_size("grp")
    col_start = lax.axis_index(OUT) * width
    local_sides = jnp.concatenate([activations, out_grads], axis=1)
    whole_sides = spread(local_sides)
    grads_whole = whole_sides[:, blocks:, :]
    weight_rows = weight.reshape(blocks, width, blocks, block)
    input_grad = jnp.einsum(
        "tjq,bcjq->tbc", grads_whole, weight_rows, preferred_element_type=jnp.float32
    ).astype(jnp.bfloat16)
    rows = block // lax.axis_size("tok")
    row_start = lax.axis_index("tok") * rows
    paired = whole_sides.reshape(tok_dev, 2, blocks, block)
    own_cols = local_sides.reshape(tok_dev, 2, blocks, width)

    def side_terms(start, span):

        def one_group(group):
            side = group % 2
            piece = group // 2
            row_part = lax.dynamic_slice(
                paired, (0, side, 0, piece * rows), (tok_dev, 1, blocks, rows)
            )[:, 0]
            col_part = lax.dynamic_slice(own_cols, (0, side, 0, 0), (tok_dev, 1, blocks, width))[
                :, 0
            ]
            return jnp.einsum(
                "tbr,tbc->rbc", row_part, col_part, preferred_element_type=jnp.float32
            )

        groups = jnp.arange(span // rows, dtype=jnp.int32)
        return lax.map(one_group, groups).reshape(span, blocks, width)

    sums = token_sums(side_terms, rows)
    tile = sums / token_count + DAMPING * diagonal_mask(rows, width, row_start, col_start)
    roots = inverse_roots(tile, row_start, col_start, owner_rows, owner_total)
    own_band = owner_rows(roots)
    other_band = swapped(own_band, "grp", 0)
    first_side = lax.axis_index("grp") == 0
    bands = jnp.concatenate(
        [jnp.where(first_side, own_band, other_band), jnp.where(first_side, other_band, own_band)],
        axis=1,
    )
    whitened = jnp.einsum(
        "tkj,jkc->tkc", whole_sides, bands, preferred_element_type=jnp.float32
    ).astype(jnp.bfloat16)
    acts_whole = spread(whitened[:, :blocks, :]).reshape(tok_dev, blocks * block)
    grads_low = whitened[:, blocks:, :]
    owned_acts = lax.all_to_all(acts_whole, ("tok", "grp"), split_axis=1, concat_axis=0, tiled=True)
    update = jnp.einsum(
        "ta,tbc->abc",
        owned_acts,
        gather_directly(grads_low, ("tok", "grp"), 0),
        preferred_element_type=jnp.float32,
    )
    update = (update / math.sqrt(token_count)).astype(jnp.bfloat16)
    return (update, input_grad)


def solution(mesh):
    split = Mesh(
        mesh.devices.reshape(mesh.shape["tok"], 2, 4, 2, mesh.shape["grp"]),
        ("tok", "out_0", "out_1", "out_2", "grp"),
    )
    in_specs = (P(("tok", "grp"), None, OUT), P(("tok", "grp"), None, OUT), P(None, OUT, None))
    out_specs = (P(("tok", "grp"), None, OUT), P(("tok", "grp"), None, OUT))
    return jax.shard_map(local, mesh=split, in_specs=in_specs, out_specs=out_specs, check_vma=False)
```

profile of v0, /device:TPU:2, one launch (start us, length us, event | category | flops | bytes accessed | tf_op | source)
XLA Modules:
  0.0 650.0 jit_solution(17056723738061298160)
XLA Ops:
  9.7 43.1 %all-gather.5.cloned.1.call-done = bf16[128,4,2048]{2,0,1:T(8,128)(2,1)} async-done(((bf16[128,4,128]{2,0,1:T(8,128)(2,1)}), bf16[128,4,2048]{2,0,1:T(8,128)(2,1)}) %all-gather.5.cloned.1.call-update) | async-done | bytes 2097168 | tf_op jit(solution)/shard_map/all_gather | solution.py:49
  52.8 79.2 %while.12 = (s32[]{:T(128)}, f32[16,256,2,128]{3,1,0,2:T(8,128)}, s32[16]{0:T(128)S(1)}, bf16[128,2,2,128]{3,0,2,1:T(8,128)(2,1)}, bf16[128,2,2,2048]{3,0,2,1:T(...) while((s32[]{:T(128)}, f32[16,256,2,128]{3,1,0,2:T(8,128)}, ...), condition=%wide.region_1.2_spmd, body=%wide.region_0.1_spmd.sunk | while | flops 16777244 | bytes 1509764 | solution.py:135
  132.1 55.9 %reduce-scatter.3.cloned.1.call-done = f32[512,2,128]{2,0,1:T(8,128)} async-done(((f32[4096,2,128]{2,0,1:T(8,128)}), f32[512,2,128]{2,0,1:T(8,128)}) %reduce-scatter.3.cloned.1.call-update) | async-done | bytes 524304 | tf_op jit(solution)/shard_map/reduce_scatter | solution.py:17
  188.2 22.1 %reduce-scatter.5.cloned.1.call-done = f32[256,2,128]{2,0,1:T(8,128)} async-done(((f32[512,2,128]{2,0,1:T(8,128)}), f32[256,2,128]{2,0,1:T(8,128)}) %reduce-scatter.5.cloned.1.call-update) | async-done | bytes 262160 | tf_op jit(solution)/shard_map/reduce_scatter | solution.py:17
  211.7 30.2 %psum.84 = f32[2,2048]{1,0:T(2,128)S(1)} all-reduce(f32[2,2048]{1,0:T(2,128)S(1)} %bitcast_dynamic-update-slice_fusion.2), channel_id=1, replica_groups=mesh['tok'=8,'out_0'=2,'out_1'=4,'out_2'=2,'grp'=2] {'tok'}, use_global_device_ids=true, to_apply=%region_4.5 | all-reduce | flops 4096 | bytes 32768 | tf_op jit(solution)/shard_map/psum | solution.py:40
  241.9 7.2 %psum.85 = f32[2,2048]{1,0:T(2,128)S(1)} all-reduce(f32[2,2048]{1,0:T(2,128)S(1)} %psum.84), channel_id=1, replica_groups=mesh['tok'=8,'out_0'=2,'out_1'=4,'out_2'=2,'grp'=2] {'out_0'}, use_global_device_ids=true, to_apply=%region_5.6 | all-reduce | flops 4096 | bytes 32768 | tf_op jit(solution)/shard_map/psum | solution.py:40
  249.1 13.9 %psum.86 = f32[2,2048]{1,0:T(2,128)S(1)} all-reduce(f32[2,2048]{1,0:T(2,128)S(1)} %psum.85), channel_id=1, replica_groups=mesh['tok'=8,'out_0'=2,'out_1'=4,'out_2'=2,'grp'=2] {'out_1'}, use_global_device_ids=true, to_apply=%region_6.7 | all-reduce | flops 4096 | bytes 32768 | tf_op jit(solution)/shard_map/psum | solution.py:40
  263.0 3.3 psum.87
  267.9 27.0 %psum.88 = f32[2,2048]{1,0:T(2,128)S(1)} all-reduce(f32[2,2048]{1,0:T(2,128)S(1)} %bitcast_dynamic-update-slice_fusion.1), channel_id=1, replica_groups=mesh['tok'=8,'out_0'=2,'out_1'=4,'out_2'=2,'grp'=2] {'tok'}, use_global_device_ids=true, to_apply=%region_9.10 | all-reduce | flops 4096 | bytes 32768 | tf_op jit(solution)/shard_map/psum | solution.py:40
  295.0 8.1 %psum.89 = f32[2,2048]{1,0:T(2,128)S(1)} all-reduce(f32[2,2048]{1,0:T(2,128)S(1)} %psum.88), channel_id=1, replica_groups=mesh['tok'=8,'out_0'=2,'out_1'=4,'out_2'=2,'grp'=2] {'out_0'}, use_global_device_ids=true, to_apply=%region_10.11 | all-reduce | flops 4096 | bytes 32768 | tf_op jit(solution)/shard_map/psum | solution.py:40
  303.1 16.4 %psum.90 = f32[2,2048]{1,0:T(2,128)S(1)} all-reduce(f32[2,2048]{1,0:T(2,128)S(1)} %psum.89), channel_id=1, replica_groups=mesh['tok'=8,'out_0'=2,'out_1'=4,'out_2'=2,'grp'=2] {'out_1'}, use_global_device_ids=true, to_apply=%region_11.12 | all-reduce | flops 4096 | bytes 32768 | tf_op jit(solution)/shard_map/psum | solution.py:40
  324.4 27.6 %psum.92 = f32[2,2048]{1,0:T(2,128)S(1)} all-reduce(f32[2,2048]{1,0:T(2,128)S(1)} %bitcast_dynamic-update-slice_fusion), channel_id=1, replica_groups=mesh['tok'=8,'out_0'=2,'out_1'=4,'out_2'=2,'grp'=2] {'tok'}, use_global_device_ids=true, to_apply=%region_14.15 | all-reduce | flops 4096 | bytes 32768 | tf_op jit(solution)/shard_map/psum | solution.py:40
  352.0 7.2 %psum.93 = f32[2,2048]{1,0:T(2,128)S(1)} all-reduce(f32[2,2048]{1,0:T(2,128)S(1)} %psum.92), channel_id=1, replica_groups=mesh['tok'=8,'out_0'=2,'out_1'=4,'out_2'=2,'grp'=2] {'out_0'}, use_global_device_ids=true, to_apply=%region_15.16 | all-reduce | flops 4096 | bytes 32768 | tf_op jit(solution)/shard_map/psum | solution.py:40
  359.2 14.3 %psum.94 = f32[2,2048]{1,0:T(2,128)S(1)} all-reduce(f32[2,2048]{1,0:T(2,128)S(1)} %psum.93), channel_id=1, replica_groups=mesh['tok'=8,'out_0'=2,'out_1'=4,'out_2'=2,'grp'=2] {'out_1'}, use_global_device_ids=true, to_apply=%region_16.17 | all-reduce | flops 4096 | bytes 32768 | tf_op jit(solution)/shard_map/psum | solution.py:40
  380.0 33.4 %all_to_all.41 = bf16[8,256,2,128]{1,3,2,0:T(8,128)(2,1)S(1)} all-to-all(bf16[8,256,2,128]{1,3,2,0:T(8,128)(2,1)S(1)} %broadcast_in_dim.58), channel_id=1, replica_groups=mesh['tok'=8,'out_0'=2,'out_1'=4,'out_2'=2,'grp'=2] {'tok'}, dimensions={0} | all-to-all | bytes 2097152 | tf_op jit(solution)/shard_map/all_to_all | solution.py:29
  419.5 35.9 %all_to_all.42 = bf16[8,256,2,128]{1,3,2,0:T(8,128)(2,1)S(1)} all-to-all(bf16[8,256,2,128]{1,3,2,0:T(8,128)(2,1)S(1)} %broadcast_in_dim.57), channel_id=1, replica_groups=mesh['tok'=8,'out_0'=2,'out_1'=4,'out_2'=2,'grp'=2] {'tok'}, dimensions={0} | all-to-all | bytes 2097152 | tf_op jit(solution)/shard_map/all_to_all | solution.py:29
  458.5 36.1 %all_to_all.43 = bf16[8,256,2,128]{1,3,2,0:T(8,128)(2,1)S(1)} all-to-all(bf16[8,256,2,128]{1,3,2,0:T(8,128)(2,1)S(1)} %broadcast_in_dim.59), channel_id=1, replica_groups=mesh['tok'=8,'out_0'=2,'out_1'=4,'out_2'=2,'grp'=2] {'tok'}, dimensions={0} | all-to-all | bytes 2097152 | tf_op jit(solution)/shard_map/all_to_all | solution.py:29
  495.7 31.0 %all_to_all.44 = bf16[8,256,2,128]{1,3,2,0:T(8,128)(2,1)S(1)} all-to-all(bf16[8,256,2,128]{1,3,2,0:T(8,128)(2,1)S(1)} %broadcast_in_dim.60), channel_id=1, replica_groups=mesh['tok'=8,'out_0'=2,'out_1'=4,'out_2'=2,'grp'=2] {'tok'}, dimensions={0} | all-to-all | bytes 2097152 | tf_op jit(solution)/shard_map/all_to_all | solution.py:29
  529.7 21.7 %collective-permute-done = bf16[2048,2,128]{0,2,1:T(8,128)(2,1)S(1)} collective-permute-done((bf16[2048,2,128]{0,2,1:T(8,128)(2,1)S(1)}, bf16[2048,2,128]{0,2,1:T(8,128)(2,1)S(1)}, u32[]{:S(2)}, u32[]{:S(2)}) %collective-permute-start) | collective-permute-done | bytes 1048608 | tf_op jit(solution)/shard_map/ppermute | solution.py:45
  554.2 5.5 all-to-all-start.5
  560.3 27.3 %all-to-all-done.5 = bf16[16,128,2,128]{3,1,2,0:T(8,128)(2,1)S(1)} async-done(((bf16[16,128,2,128]{3,1,2,0:T(8,128)(2,1)}), bf16[16,128,2,128]{3,1,2,0:T(8,128)(2,1)S(1)}, u32[]{:S(2)}, u32[]{:S(2)}) %all-to-all-start.5) | async-done | bytes 1048608 | tf_op jit(solution)/shard_map/all_to_all | solution.py:29
  587.6 13.5 %all-gather.11.cloned.1.call-done = bf16[128,2,2048]{0,2,1:T(8,128)(2,1)} async-done(((bf16[128,2,128]{0,2,1:T(8,128)(2,1)}), bf16[128,2,2048]{0,2,1:T(8,128)(2,1)}) %all-gather.11.cloned.1.call-update) | async-done | bytes 1048592 | tf_op jit(solution)/shard_map/all_gather | solution.py:49
  601.0 10.3 %all-to-all-start.4 = ((bf16[128,16,256]{0,2,1:T(8,128)(2,1)}), bf16[128,16,256]{0,2,1:T(8,128)(2,1)S(1)}, u32[]{:S(2)}, u32[]{:S(2)}) async-start(bf16[128,16,256]{0,2,1:T(8,128)(2,1)} %bitcast.112), calls=%async_computation.6 | async-start | bytes 2097152 | tf_op jit(solution)/shard_map/all_to_all | solution.py:152
  614.8 27.2 %all-to-all-done.4 = bf16[128,16,256]{0,2,1:T(8,128)(2,1)S(1)} async-done(((bf16[128,16,256]{0,2,1:T(8,128)(2,1)}), bf16[128,16,256]{0,2,1:T(8,128)(2,1)S(1)}, u32[]{:S(2)}, u32[]{:S(2)}) %all-to-all-start.4) | async-done | bytes 1048608 | tf_op jit(solution)/shard_map/all_to_all | solution.py:152
  (137 shorter events, 79.9 us)
Async XLA Ops:
  7.2 45.6 %all-gather.5.cloned.1.call-start = ((), (), s32[]{:S(2)}) async-start(), calls=%async_computation.8 | async-start | bytes 2228224 | tf_op jit(solution)/shard_map/all_gather | solution.py:49
  8.9 0.7 copy-start.1
  9.6 178.4 %reduce-scatter.3.cloned.1.call-start = ((), (), s32[]{:S(2)}) async-start(), calls=%async_computation.9 | async-start | bytes 4718592 | tf_op jit(solution)/shard_map/reduce_scatter | solution.py:17
  132.0 78.3 %reduce-scatter.5.cloned.1.call-start = ((), (), s32[]{:S(2)}) async-start(), calls=%async_computation.10 | async-start | bytes 786432 | tf_op jit(solution)/shard_map/reduce_scatter | solution.py:17
  188.0 228.1 %all-gather.7.cloned.1.call-start = ((), (), s32[]{:S(2)}) async-start(), calls=%async_computation.11 | async-start | bytes 2228224 | tf_op jit(solution)/shard_map/all_gather | solution.py:49
  378.8 76.9 %all-gather.9.cloned.1.call-start = ((), (), s32[]{:S(2)}) async-start(), calls=%async_computation.12 | async-start | bytes 2228224 | tf_op jit(solution)/shard_map/all_gather | solution.py:49
  458.5 36.2 %copy-start = (bf16[256,2,2048]{2,0,1:T(8,128)(2,1)S(1)}, bf16[256,2,2048]{2,0,1:T(8,128)(2,1)}, u32[]{:S(2)}) copy-start(bf16[256,2,2048]{2,0,1:T(8,128)(2,1)} %all-gather.7.cloned.1.call-done) | copy-start | bytes 6291460
  526.8 24.5 %collective-permute-start = (bf16[2048,2,128]{0,2,1:T(8,128)(2,1)S(1)}, bf16[2048,2,128]{0,2,1:T(8,128)(2,1)S(1)}, u32[]{:S(2)}, u32[]{:S(2)}) collective-permute-start(bf16[2048,2,128]{0,2,1:T(8,128)(2,1)S(1)} %bitcast.102), channel_id=1, source_target_pairs={{0,1},{1,0},{2,3},{3,2},{4,5},{5,4},{6,7},{7,6},{8,9},{9,8},{10,11... | collective-permute-start | bytes 3145736 | tf_op jit(solution)/shard_map/ppermute | solution.py:45
  529.7 21.8 %copy-start.2 = (bf16[128,2,2,2048]{3,0,2,1:T(8,128)(2,1)S(1)}, bf16[128,2,2,2048]{3,0,2,1:T(8,128)(2,1)}, u32[]{:S(2)}) copy-start(bf16[128,2,2,2048]{3,0,2,1:T(8,128)(2,1)} %get-tuple-element.215) | copy-start | bytes 6291460
  554.2 33.3 %all-to-all-start.5 = ((bf16[16,128,2,128]{3,1,2,0:T(8,128)(2,1)}), bf16[16,128,2,128]{3,1,2,0:T(8,128)(2,1)S(1)}, u32[]{:S(2)}, u32[]{:S(2)}) async-start(bf16[16,128,2,128]{3,1,2,0:T(8,128)(2,1)} %broadcast_in_dim.61), calls=%async_computation.7 | async-start | bytes 2097152 | tf_op jit(solution)/shard_map/all_to_all | solution.py:29
  559.7 41.3 %all-gather.11.cloned.1.call-start = ((), (), s32[]{:S(2)}) async-start(), calls=%async_computation.13 | async-start | bytes 1114112 | tf_op jit(solution)/shard_map/all_gather | solution.py:49
  601.0 40.9 %all-to-all-start.4 = ((bf16[128,16,256]{0,2,1:T(8,128)(2,1)}), bf16[128,16,256]{0,2,1:T(8,128)(2,1)S(1)}, u32[]{:S(2)}, u32[]{:S(2)}) async-start(bf16[128,16,256]{0,2,1:T(8,128)(2,1)} %bitcast.112), calls=%async_computation.6 | async-start | bytes 2097152 | tf_op jit(solution)/shard_map/all_to_all | solution.py:152
Sparse Core Ops, SparseCore 0:
  10.3 42.3 all-gather.4
  132.1 55.8 reduce-scatter.2
  190.5 19.7 reduce-scatter.4
  378.9 37.1 all-gather.6
  419.4 36.2 all-gather.8
  562.8 38.2 all-gather.10
where the time goes:
time: 652 us; the launch traced here: 650 us
  blocking collectives  298 us (46%)
  waiting for transfers between devices  214 us (33%)
  loops' own time  37.5 us (6%)
  matrix products  33 us (5%)
  local copies, waits for them, and re-layouts  31.1 us (5%)
  starting transfers between devices  18.8 us (3%)
  between operations  14.4 us (2%)
    psum x12, blocking collectives, one_axis_at_a_time(): array = lax.psum(array, axis)  162 us
    all_to_all x4, blocking collectives, copy_for_each(): lax.all_to_all(jnp.broadcast_to(array[None], (peers, *array.shape)), axis...  136 us
    reduce_scatter x2, waiting for transfers between devices, own_rows(): so_far = lax.psum_scatter(so_far, axis, scatter_dimension=0, tiled=True)  78.1 us
    all_gather x4, waiting for transfers between devices, spread(): return lax.all_gather(piece, OUT, axis=2, tiled=True)  59.4 us
    another operation x1, loops' own time, side_terms(): return lax.map(one_group, groups).reshape(span, blocks, width)  37.5 us
    all_to_all x1, waiting for transfers between devices, copy_for_each(): lax.all_to_all(jnp.broadcast_to(array[None], (peers, *array.shape)), axis...  27.3 us
    all_to_all x1, waiting for transfers between devices, local(): lax.all_to_all(acts_whole, ('tok', 'grp'), split_axis=1, concat_axis=0, t...  27.2 us
    ppermute x1, waiting for transfers between devices, swapped(): lax.ppermute(array, axis, [(i, i ^ 1 << stride) for i in range(lax.axis_s...  21.7 us
  transfers between devices with their start and end apart: 9, of which 9 were waited for; matrix products, arithmetic and copies ran while one was open for 1% of the time, Pallas kernels for 0%

commit v1 on v0

--- a/solution.py
+++ b/solution.py
@@ -37,7 +37,7 @@
 
 def one_axis_at_a_time(array, axes):
     for axis in axes:
-        array = lax.psum(array, axis)
+        array = jnp.sum(lax.all_gather(array, axis), axis=0)
     return array
 
 

time: 652 us -> 618 us (0.948)
  blocking collectives: 298 us -> 267 us
    psum x12 -> x0, blocking collectives: 162 us -> none  [one_axis_at_a_time(): array = lax.psum(array, axis)]
    all_gather x0 -> x12, blocking collectives: none -> 130 us  [one_axis_at_a_time(): array = jnp.sum(lax.all_gather(array, axis), axis=0)]
where the time goes in v1:
time: 618 us; the launch traced here: 616 us
  blocking collectives  267 us (43%)
  waiting for transfers between devices  213 us (34%)
  loops' own time  37.5 us (6%)
  matrix products  32.1 us (5%)
  local copies, waits for them, and re-layouts  31.1 us (5%)
  starting transfers between devices  18.8 us (3%)
  between operations  14.4 us (2%)
    all_to_all x4, blocking collectives, copy_for_each(): lax.all_to_all(jnp.broadcast_to(array[None], (peers, *array.shape)), axis...  138 us
    all_gather x12, blocking collectives, one_axis_at_a_time(): array = jnp.sum(lax.all_gather(array, axis), axis=0)  130 us
    reduce_scatter x2, waiting for transfers between devices, own_rows(): so_far = lax.psum_scatter(so_far, axis, scatter_dimension=0, tiled=True)  78.1 us
    all_gather x4, waiting for transfers between devices, spread(): return lax.all_gather(piece, OUT, axis=2, tiled=True)  58.6 us
    another operation x1, loops' own time, side_terms(): return lax.map(one_group, groups).reshape(span, blocks, width)  37.5 us
    all_to_all x1, waiting for transfers between devices, copy_for_each(): lax.all_to_all(jnp.broadcast_to(array[None], (peers, *array.shape)), axis...  27.3 us
    all_to_all x1, waiting for transfers between devices, local(): lax.all_to_all(acts_whole, ('tok', 'grp'), split_axis=1, concat_axis=0, t...  27.2 us
    ppermute x1, waiting for transfers between devices, swapped(): lax.ppermute(array, axis, [(i, i ^ 1 << stride) for i in range(lax.axis_s...  21.6 us
  transfers between devices with their start and end apart: 9, of which 9 were waited for; matrix products, arithmetic and copies ran while one was open for 1% of the time, Pallas kernels for 0%

profile of v1, /device:TPU:2, one launch (start us, length us, event | category | flops | bytes accessed | tf_op | source)
XLA Modules:
  0.0 616.4 jit_solution(6681882134788316795)
XLA Ops:
  9.7 43.1 %all-gather.23.cloned.1.call-done = bf16[128,4,2048]{2,0,1:T(8,128)(2,1)} async-done(((bf16[128,4,128]{2,0,1:T(8,128)(2,1)}), bf16[128,4,2048]{2,0,1:T(8,128)(2,1)}) %all-gather.23.cloned.1.call-update) | async-done | bytes 2097168 | tf_op jit(solution)/shard_map/all_gather | solution.py:49
  52.8 79.2 %while.12 = (s32[]{:T(128)}, f32[16,256,2,128]{3,1,0,2:T(8,128)}, s32[16]{0:T(128)S(1)}, bf16[128,2,2,128]{3,0,2,1:T(8,128)(2,1)}, bf16[128,2,2,2048]{3,0,2,1:T(...) while((s32[]{:T(128)}, f32[16,256,2,128]{3,1,0,2:T(8,128)}, ...), condition=%wide.region_1.2_spmd, body=%wide.region_0.1_spmd.sunk | while | flops 16777244 | bytes 1509764 | solution.py:135
  132.1 55.9 %reduce-scatter.3.cloned.1.call-done = f32[512,2,128]{2,0,1:T(8,128)} async-done(((f32[4096,2,128]{2,0,1:T(8,128)}), f32[512,2,128]{2,0,1:T(8,128)}) %reduce-scatter.3.cloned.1.call-update) | async-done | bytes 524304 | tf_op jit(solution)/shard_map/reduce_scatter | solution.py:17
  188.2 22.1 %reduce-scatter.5.cloned.1.call-done = f32[256,2,128]{2,0,1:T(8,128)} async-done(((f32[512,2,128]{2,0,1:T(8,128)}), f32[256,2,128]{2,0,1:T(8,128)}) %reduce-scatter.5.cloned.1.call-update) | async-done | bytes 262160 | tf_op jit(solution)/shard_map/reduce_scatter | solution.py:17
  211.8 26.0 %all_gather.90 = f32[8,2,2048]{2,1,0:T(2,128)S(1)} all-gather(f32[1,2,2048]{2,1,0:T(2,128)S(1)} %bitcast_dynamic-update-slice_fusion.2), channel_id=1, replica_groups=mesh['tok'=8,'out_0'=2,'out_1'=4,'out_2'=2,'grp'=2] {'tok'}, dimensions={0}, use_global_device_ids=true | all-gather | bytes 147456 | tf_op jit(solution)/shard_map/all_gather | solution.py:40
  237.8 4.4 all-gather.9
  242.3 11.9 %all-gather.10 = f32[4,2,2048]{2,1,0:T(2,128)S(1)} all-gather(f32[1,2,2048]{2,1,0:T(2,128)S(1)} %bitcast.130), channel_id=3, replica_groups=mesh['tok'=8,'out_0'=2,'out_1'=4,'out_2'=2,'grp'=2] {'out_1'}, dimensions={0}, use_global_device_ids=true | all-gather | bytes 81920 | tf_op jit(solution)/shard_map/all_gather | solution.py:40
  257.6 24.6 %all_gather.98 = f32[8,2,2048]{2,1,0:T(2,128)S(1)} all-gather(f32[1,2,2048]{2,1,0:T(2,128)S(1)} %bitcast_dynamic-update-slice_fusion.1), channel_id=1, replica_groups=mesh['tok'=8,'out_0'=2,'out_1'=4,'out_2'=2,'grp'=2] {'tok'}, dimensions={0}, use_global_device_ids=true | all-gather | bytes 147456 | tf_op jit(solution)/shard_map/all_gather | solution.py:40
  282.2 4.4 all-gather.12
  286.7 11.9 %all-gather.13 = f32[4,2,2048]{2,1,0:T(2,128)S(1)} all-gather(f32[1,2,2048]{2,1,0:T(2,128)S(1)} %bitcast.133), channel_id=6, replica_groups=mesh['tok'=8,'out_0'=2,'out_1'=4,'out_2'=2,'grp'=2] {'out_1'}, dimensions={0}, use_global_device_ids=true | all-gather | bytes 81920 | tf_op jit(solution)/shard_map/all_gather | solution.py:40
  301.0 24.6 %all_gather.106 = f32[8,2,2048]{2,1,0:T(2,128)S(1)} all-gather(f32[1,2,2048]{2,1,0:T(2,128)S(1)} %bitcast_dynamic-update-slice_fusion), channel_id=1, replica_groups=mesh['tok'=8,'out_0'=2,'out_1'=4,'out_2'=2,'grp'=2] {'tok'}, dimensions={0}, use_global_device_ids=true | all-gather | bytes 147456 | tf_op jit(solution)/shard_map/all_gather | solution.py:40
  325.7 4.4 all-gather.15
  330.1 11.9 %all-gather.16 = f32[4,2,2048]{2,1,0:T(2,128)S(1)} all-gather(f32[1,2,2048]{2,1,0:T(2,128)S(1)} %bitcast.136), channel_id=9, replica_groups=mesh['tok'=8,'out_0'=2,'out_1'=4,'out_2'=2,'grp'=2] {'out_1'}, dimensions={0}, use_global_device_ids=true | all-gather | bytes 81920 | tf_op jit(solution)/shard_map/all_gather | solution.py:40
  346.0 34.5 %all_to_all.41 = bf16[8,256,2,128]{1,3,2,0:T(8,128)(2,1)S(1)} all-to-all(bf16[8,256,2,128]{1,3,2,0:T(8,128)(2,1)S(1)} %broadcast_in_dim.58), channel_id=1, replica_groups=mesh['tok'=8,'out_0'=2,'out_1'=4,'out_2'=2,'grp'=2] {'tok'}, dimensions={0} | all-to-all | bytes 2097152 | tf_op jit(solution)/shard_map/all_to_all | solution.py:29
  382.4 3.1 fusion.21
  385.8 35.9 %all_to_all.42 = bf16[8,256,2,128]{1,3,2,0:T(8,128)(2,1)S(1)} all-to-all(bf16[8,256,2,128]{1,3,2,0:T(8,128)(2,1)S(1)} %broadcast_in_dim.57), channel_id=1, replica_groups=mesh['tok'=8,'out_0'=2,'out_1'=4,'out_2'=2,'grp'=2] {'tok'}, dimensions={0} | all-to-all | bytes 2097152 | tf_op jit(solution)/shard_map/all_to_all | solution.py:29
  424.9 36.1 %all_to_all.43 = bf16[8,256,2,128]{1,3,2,0:T(8,128)(2,1)S(1)} all-to-all(bf16[8,256,2,128]{1,3,2,0:T(8,128)(2,1)S(1)} %broadcast_in_dim.59), channel_id=1, replica_groups=mesh['tok'=8,'out_0'=2,'out_1'=4,'out_2'=2,'grp'=2] {'tok'}, dimensions={0} | all-to-all | bytes 2097152 | tf_op jit(solution)/shard_map/all_to_all | solution.py:29
  462.0 31.0 %all_to_all.44 = bf16[8,256,2,128]{1,3,2,0:T(8,128)(2,1)S(1)} all-to-all(bf16[8,256,2,128]{1,3,2,0:T(8,128)(2,1)S(1)} %broadcast_in_dim.60), channel_id=1, replica_groups=mesh['tok'=8,'out_0'=2,'out_1'=4,'out_2'=2,'grp'=2] {'tok'}, dimensions={0} | all-to-all | bytes 2097152 | tf_op jit(solution)/shard_map/all_to_all | solution.py:29
  496.0 21.6 %collective-permute-done = bf16[2048,2,128]{0,2,1:T(8,128)(2,1)S(1)} collective-permute-done((bf16[2048,2,128]{0,2,1:T(8,128)(2,1)S(1)}, bf16[2048,2,128]{0,2,1:T(8,128)(2,1)S(1)}, u32[]{:S(2)}, u32[]{:S(2)}) %collective-permute-start) | collective-permute-done | bytes 1048608 | tf_op jit(solution)/shard_map/ppermute | solution.py:45
  520.6 5.5 all-to-all-start.5
  526.7 27.3 %all-to-all-done.5 = bf16[16,128,2,128]{3,1,2,0:T(8,128)(2,1)S(1)} async-done(((bf16[16,128,2,128]{3,1,2,0:T(8,128)(2,1)}), bf16[16,128,2,128]{3,1,2,0:T(8,128)(2,1)S(1)}, u32[]{:S(2)}, u32[]{:S(2)}) %all-to-all-start.5) | async-done | bytes 1048608 | tf_op jit(solution)/shard_map/all_to_all | solution.py:29
  553.9 13.5 %all-gather.29.cloned.1.call-done = bf16[128,2,2048]{0,2,1:T(8,128)(2,1)} async-done(((bf16[128,2,128]{0,2,1:T(8,128)(2,1)}), bf16[128,2,2048]{0,2,1:T(8,128)(2,1)}) %all-gather.29.cloned.1.call-update) | async-done | bytes 1048592 | tf_op jit(solution)/shard_map/all_gather | solution.py:49
  567.4 10.3 %all-to-all-start.4 = ((bf16[128,16,256]{0,2,1:T(8,128)(2,1)}), bf16[128,16,256]{0,2,1:T(8,128)(2,1)S(1)}, u32[]{:S(2)}, u32[]{:S(2)}) async-start(bf16[128,16,256]{0,2,1:T(8,128)(2,1)} %bitcast.124), calls=%async_computation.6 | async-start | bytes 2097152 | tf_op jit(solution)/shard_map/all_to_all | solution.py:152
  581.2 27.2 %all-to-all-done.4 = bf16[128,16,256]{0,2,1:T(8,128)(2,1)S(1)} async-done(((bf16[128,16,256]{0,2,1:T(8,128)(2,1)}), bf16[128,16,256]{0,2,1:T(8,128)(2,1)S(1)}, u32[]{:S(2)}, u32[]{:S(2)}) %all-to-all-start.4) | async-done | bytes 1048608 | tf_op jit(solution)/shard_map/all_to_all | solution.py:152
  (151 shorter events, 73.3 us)
Async XLA Ops:
  7.2 45.6 %all-gather.23.cloned.1.call-start = ((), (), s32[]{:S(2)}) async-start(), calls=%async_computation.8 | async-start | bytes 2228224 | tf_op jit(solution)/shard_map/all_gather | solution.py:49
  8.9 0.7 copy-start.2
  9.6 178.4 %reduce-scatter.3.cloned.1.call-start = ((), (), s32[]{:S(2)}) async-start(), calls=%async_computation.9 | async-start | bytes 4718592 | tf_op jit(solution)/shard_map/reduce_scatter | solution.py:17
  132.0 78.3 %reduce-scatter.5.cloned.1.call-start = ((), (), s32[]{:S(2)}) async-start(), calls=%async_computation.10 | async-start | bytes 786432 | tf_op jit(solution)/shard_map/reduce_scatter | solution.py:17
  188.0 194.4 %all-gather.25.cloned.1.call-start = ((), (), s32[]{:S(2)}) async-start(), calls=%async_computation.11 | async-start | bytes 2228224 | tf_op jit(solution)/shard_map/all_gather | solution.py:49
  210.3 90.3 %copy-start = (f32[256,2,128]{2,0,1:T(8,128)S(1)}, f32[256,2,128]{2,0,1:T(8,128)}, u32[]{:S(2)}) copy-start(f32[256,2,128]{2,0,1:T(8,128)} %reduce-scatter.5.cloned.1.call-done) | copy-start | bytes 786436
  344.9 77.2 %all-gather.27.cloned.1.call-start = ((), (), s32[]{:S(2)}) async-start(), calls=%async_computation.12 | async-start | bytes 2228224 | tf_op jit(solution)/shard_map/all_gather | solution.py:49
  424.9 36.2 %copy-start.1 = (bf16[256,2,2048]{2,0,1:T(8,128)(2,1)S(1)}, bf16[256,2,2048]{2,0,1:T(8,128)(2,1)}, u32[]{:S(2)}) copy-start(bf16[256,2,2048]{2,0,1:T(8,128)(2,1)} %all-gather.25.cloned.1.call-done) | copy-start | bytes 6291460
  493.2 24.5 %collective-permute-start = (bf16[2048,2,128]{0,2,1:T(8,128)(2,1)S(1)}, bf16[2048,2,128]{0,2,1:T(8,128)(2,1)S(1)}, u32[]{:S(2)}, u32[]{:S(2)}) collective-permute-start(bf16[2048,2,128]{0,2,1:T(8,128)(2,1)S(1)} %bitcast.114), channel_id=1, source_target_pairs={{0,1},{1,0},{2,3},{3,2},{4,5},{5,4},{6,7},{7,6},{8,9},{9,8},{10,11... | collective-permute-start | bytes 3145736 | tf_op jit(solution)/shard_map/ppermute | solution.py:45
  496.0 21.8 %copy-start.3 = (bf16[128,2,2,2048]{3,0,2,1:T(8,128)(2,1)S(1)}, bf16[128,2,2,2048]{3,0,2,1:T(8,128)(2,1)}, u32[]{:S(2)}) copy-start(bf16[128,2,2,2048]{3,0,2,1:T(8,128)(2,1)} %get-tuple-element.215) | copy-start | bytes 6291460
  520.6 33.3 %all-to-all-start.5 = ((bf16[16,128,2,128]{3,1,2,0:T(8,128)(2,1)}), bf16[16,128,2,128]{3,1,2,0:T(8,128)(2,1)S(1)}, u32[]{:S(2)}, u32[]{:S(2)}) async-start(bf16[16,128,2,128]{3,1,2,0:T(8,128)(2,1)} %broadcast_in_dim.61), calls=%async_computation.7 | async-start | bytes 2097152 | tf_op jit(solution)/shard_map/all_to_all | solution.py:29
  526.1 41.3 %all-gather.29.cloned.1.call-start = ((), (), s32[]{:S(2)}) async-start(), calls=%async_computation.13 | async-start | bytes 1114112 | tf_op jit(solution)/shard_map/all_gather | solution.py:49
  567.4 40.9 %all-to-all-start.4 = ((bf16[128,16,256]{0,2,1:T(8,128)(2,1)}), bf16[128,16,256]{0,2,1:T(8,128)(2,1)S(1)}, u32[]{:S(2)}, u32[]{:S(2)}) async-start(bf16[128,16,256]{0,2,1:T(8,128)(2,1)} %bitcast.124), calls=%async_computation.6 | async-start | bytes 2097152 | tf_op jit(solution)/shard_map/all_to_all | solution.py:152
Sparse Core Ops, SparseCore 0:
  10.3 42.3 all-gather.22
  132.1 55.8 reduce-scatter.2
  190.5 19.7 reduce-scatter.4
  345.0 37.3 all-gather.24
  385.7 36.3 all-gather.26
  529.1 38.2 all-gather.28
